TPU v7x, 256 devices: a whole 4x4x8 slice. The times are simulated.
256 devices in a mesh: gx: 32 (over y, z_lo, core), gy: 8 (over z_hi, x).
Axes of the slice: x: 4, y: 4, z: 8 (z_hi: 2, z_lo: 4; z = z_hi * 4 + z_lo), core: 2. Of those that a mesh axis runs over, the one named last changes fastest.
Arguments:
- features: bfloat16 [32, 8, 3, 512, 192], P('gx', 'gy'), may hold values from -6 to 6
- weight: bfloat16 [5184, 192], replicated, may hold values from -0.078125 to 0.078125
- cotangent: bfloat16 [32, 8, 3, 64, 192], P('gx', 'gy'), may hold values from -6 to 6
- valid: int32 [32, 8, 3], P('gx', 'gy'), may hold values from 0 to 1, as said below
- local_rules: int32 [32, 8, 2, 12], P('gx', 'gy'), may hold values from 0 to 3, as said below
- local_codes: int32 [32, 8, 12], P('gx', 'gy'), may hold values from 0 to 7
- remote_rules: int32 [32, 8, 2, 3, 3], P('gx', 'gy'), may hold values from 0 to 3, as said below
- remote_codes: int32 [32, 8, 3, 3], P('gx', 'gy'), may hold values from 1 to 7, as said below
Outputs:
- output: bfloat16 [32, 8, 3, 64, 192], P('gx', 'gy')
- features_grad: bfloat16 [32, 8, 3, 512, 192], P('gx', 'gy')
- weight_grad: float32 [5184, 192], P('gx')
Inputs may be any that keep to these rules, and one draw needn't show every extreme that they name: `valid`: 1 marks a live brick slot; on each device the live slots come first and at least one slot is live. `local_rules`: entry [., ., 0, e] is a source slot and [., ., 1, e] a target slot of the same device; a target 3 marks an empty entry; non-empty entries name live slots. `remote_rules`: class m (third dimension) entry: a source slot on this device and a target slot on the device one step higher along gx (m = 0), along gy (m = 1) or along both (m = 2); a target 3 marks an empty entry; non-empty entries name live slots; devices at the upper end of an axis have no non-empty entries in the classes that cross it. `remote_codes`: the offset k mod 2 is 1 in classes 0 and 2, and the offset (k // 2) mod 2 is 1 in classes 1 and 2.
All inputs are finite; a program needn't handle non-finite values.
Results may differ from a plain program's by a relative error of at most 0.0045.
Values may be sent and summed in bfloat16 or wider, within the bound.
No kernel may reach another device: no remote copies, remote signals or barrier semaphores. Data moves between devices by JAX's collectives and lax.ppermute only.
A program may use at most 128 MiB of HBM per device.

v0:
```python
from functools import partial
import jax
import jax.numpy as jnp
import numpy as np
from jax import lax
from jax.sharding import PartitionSpec as P


def shifted(block, axis, distance):
    devices = range(lax.axis_size(axis))
    route = [(i - distance, i) for i in devices if i - distance in devices]
    return lax.ppermute(block, axis, route)


def offset_table(row_x, row_y, row_z):
    code_list = np.arange(8)[:, None]
    step_x = code_list % 2
    step_y = code_list // 2 % 2
    step_z = code_list // 4
    inside = (
        ((step_x == 0) | (row_x[None, :] == 0))
        & ((step_y == 0) | (row_y[None, :] == 0))
        & ((step_z == 0) | (row_z[None, :] == 0))
    )
    source_row = (
        (row_x[None, :] + 4 * step_x) * 25
        + (row_y[None, :] + 4 * step_y) * 5
        + row_z[None, :]
        + 4 * step_z
    )
    return np.where(inside, source_row, 125).astype(np.int32)


def full_table():
    voxel_ids = np.arange(64)
    return offset_table(voxel_ids // 16, voxel_ids // 4 % 4, voxel_ids % 4)


def face_x_table():
    face_ids = np.arange(16)
    return offset_table(np.zeros(16, np.int64), face_ids // 4, face_ids % 4)


def face_y_table():
    face_ids = np.arange(16)
    return offset_table(face_ids // 4, np.zeros(16, np.int64), face_ids % 4)


def corner_table():
    edge_ids = np.arange(4)
    return offset_table(np.zeros(4, np.int64), np.zeros(4, np.int64), edge_ids)


def brick_patches(one_brick):
    channels = one_brick.shape[-1]
    cube = one_brick.reshape(8, 8, 8, channels)
    padded = jnp.pad(cube, ((1, 2), (1, 2), (1, 2), (0, 0)))
    tap_list = []
    for along_x in range(3):
        for along_y in range(3):
            for along_z in range(3):
                tap_list.append(
                    padded[
                        along_x : along_x + 9 : 2,
                        along_y : along_y + 9 : 2,
                        along_z : along_z + 9 : 2,
                        :,
                    ]
                )
    return jnp.stack(tap_list, axis=3).reshape(125, 27 * channels)


def fold_front(values):
    even_part = values[0:4, 1]
    odd_part = values[1:5, 0] + values[0:4, 2]
    stacked = jnp.stack([even_part, odd_part], axis=1)
    return stacked.reshape((8,) + stacked.shape[2:])


def brick_fold(patch_grads, channels):
    tap_grads = patch_grads.reshape(5, 5, 5, 3, 3, 3, channels)
    ordered = jnp.transpose(tap_grads, (0, 3, 1, 4, 2, 5, 6))
    along_x = fold_front(ordered)
    along_x = jnp.transpose(along_x, (1, 2, 0, 3, 4, 5))
    along_y = fold_front(along_x)
    along_y = jnp.transpose(along_y, (2, 3, 1, 0, 4))
    along_z = fold_front(along_y)
    return jnp.transpose(along_z, (1, 2, 0, 3)).reshape(512, channels)


def row_positions(sources, code_list, row_table):
    return sources[:, None] * 126 + jnp.asarray(row_table)[code_list]


def pick_float(index, table):
    flat_index = index.reshape(-1)
    hits = (flat_index[:, None] == jnp.arange(table.shape[0], dtype=jnp.int32)[None, :]).astype(
        jnp.float32
    )
    picked = jnp.dot(
        hits, table, precision=lax.Precision.HIGHEST, preferred_element_type=jnp.float32
    )
    return picked.reshape(index.shape + (table.shape[1],))


def pick_half(index, table):
    hits = (index[:, None] == jnp.arange(table.shape[0], dtype=jnp.int32)[None, :]).astype(
        jnp.bfloat16
    )
    flat_table = table.reshape(table.shape[0], -1)
    picked = jnp.dot(hits, flat_table, preferred_element_type=jnp.float32).astype(jnp.bfloat16)
    return picked.reshape((index.shape[0],) + table.shape[1:])


def collect(targets, pieces, bricks):
    hits = (targets[None, :] == jnp.arange(bricks, dtype=jnp.int32)[:, None]).astype(jnp.float32)
    flat_pieces = pieces.reshape(pieces.shape[0], -1)
    return jnp.dot(
        hits, flat_pieces, precision=lax.Precision.HIGHEST, preferred_element_type=jnp.float32
    )


def shards(
    features, weight, cotangent, valid, local_rules, local_codes, remote_rules, remote_codes
):
    bricks = features.shape[2]
    channels = features.shape[-1]
    live_slots = valid[0, 0]
    live_float = live_slots.astype(jnp.float32)[:, None, None]
    masked = features[0, 0] * live_slots.astype(jnp.bfloat16)[:, None, None]
    flat_patches = jax.vmap(brick_patches)(masked).reshape(bricks * 125, 27 * channels)
    partials = jnp.dot(flat_patches, weight, preferred_element_type=jnp.float32).reshape(
        bricks, 125, channels
    )
    zero_rows = jnp.zeros((bricks, 1, channels), jnp.float32)
    partial_rows = jnp.concatenate([partials, zero_rows], axis=1).reshape(bricks * 126, channels)
    index_x = row_positions(remote_rules[0, 0, 0, 0], remote_codes[0, 0, 0], face_x_table())
    index_y = row_positions(remote_rules[0, 0, 0, 1], remote_codes[0, 0, 1], face_y_table())
    index_xy = row_positions(remote_rules[0, 0, 0, 2], remote_codes[0, 0, 2], corner_table())
    index_local = row_positions(local_rules[0, 0, 0], local_codes[0, 0], full_table())
    target_x = remote_rules[0, 0, 1, 0]
    target_y = remote_rules[0, 0, 1, 1]
    target_xy = remote_rules[0, 0, 1, 2]
    target_local = local_rules[0, 0, 1]
    pieces_x = pick_float(index_x, partial_rows)
    pieces_y = pick_float(index_y, partial_rows)
    pieces_xy = pick_float(index_xy, partial_rows)
    got_x, got_x_target = (
        shifted(pieces_x.astype(jnp.bfloat16), "gx", 1).astype(pieces_x.dtype),
        shifted(target_x, "gx", 1),
    )
    got_y, got_y_target = (
        shifted(pieces_y.astype(jnp.bfloat16), "gy", 1).astype(pieces_y.dtype),
        shifted(target_y, "gy", 1),
    )
    middle_xy, middle_target = shifted((pieces_xy, target_xy), "gx", 1)
    got_xy, got_xy_target = shifted((middle_xy, middle_target), "gy", 1)
    local_pieces = pick_float(index_local, partial_rows)
    totals = collect(target_local, local_pieces, bricks).reshape(bricks, 4, 4, 4, channels)
    face_x_sum = collect(got_x_target, got_x, bricks).reshape(bricks, 1, 4, 4, channels)
    face_y_sum = collect(got_y_target, got_y, bricks).reshape(bricks, 4, 1, 4, channels)
    edge_sum = collect(got_xy_target, got_xy, bricks).reshape(bricks, 1, 1, 4, channels)
    totals = totals + jnp.pad(face_x_sum, ((0, 0), (0, 3), (0, 0), (0, 0), (0, 0)))
    totals = totals + jnp.pad(face_y_sum, ((0, 0), (0, 0), (0, 3), (0, 0), (0, 0)))
    totals = totals + jnp.pad(edge_sum, ((0, 0), (0, 3), (0, 3), (0, 0), (0, 0)))
    output = (totals.reshape(bricks, 64, channels) * live_float).astype(jnp.bfloat16)
    grad_out = cotangent[0, 0] * live_slots.astype(jnp.bfloat16)[:, None, None]
    grad_pad = jnp.concatenate([grad_out, jnp.zeros((1, 64, channels), jnp.bfloat16)], axis=0)
    grad_cube = grad_pad.reshape(bricks + 1, 4, 4, 4, channels)
    back_x = pick_half(got_x_target, grad_cube[:, 0].reshape(bricks + 1, 16, channels))
    back_y = pick_half(got_y_target, grad_cube[:, :, 0].reshape(bricks + 1, 16, channels))
    back_xy = pick_half(got_xy_target, grad_cube[:, 0, 0])
    return_x = shifted(back_x, "gx", -1)
    return_y = shifted(back_y, "gy", -1)
    middle_back = shifted(back_xy, "gy", -1)
    return_xy = shifted(middle_back, "gx", -1)
    index_all = jnp.concatenate(
        [index_local.reshape(-1), index_x.reshape(-1), index_y.reshape(-1), index_xy.reshape(-1)]
    )
    value_all = jnp.concatenate(
        [
            pick_half(target_local, grad_pad).reshape(-1, channels),
            return_x.reshape(-1, channels),
            return_y.reshape(-1, channels),
            return_xy.reshape(-1, channels),
        ],
        axis=0,
    )
    row_hits = (jnp.arange(bricks * 126, dtype=jnp.int32)[:, None] == index_all[None, :]).astype(
        jnp.bfloat16
    )
    grad_rows = jnp.dot(row_hits, value_all, preferred_element_type=jnp.float32)
    grad_rounded = grad_rows.reshape(bricks, 126, channels)[:, :125].astype(jnp.bfloat16)
    flat_grads = grad_rounded.reshape(bricks * 125, channels)
    patch_grads = lax.dot_general(
        flat_grads, weight, (((1,), (1,)), ((), ())), preferred_element_type=jnp.float32
    )
    weight_local = lax.dot_general(
        flat_patches, flat_grads, (((0,), (0,)), ((), ())), preferred_element_type=jnp.float32
    )
    folded = jax.vmap(partial(brick_fold, channels=channels))(
        patch_grads.reshape(bricks, 125, 27 * channels)
    )
    features_grad = (folded * live_float).astype(jnp.bfloat16)
    summed = lax.psum(weight_local, ("gx", "gy"))
    share_rows = summed.shape[0] // lax.axis_size("gx")
    weight_share = lax.dynamic_slice_in_dim(
        summed, lax.axis_index("gx") * share_rows, share_rows, 0
    )
    return (output[None, None], features_grad[None, None], weight_share)


def solution(mesh):
    return jax.shard_map(
        shards,
        mesh=mesh,
        in_specs=(
            P("gx", "gy", None, None, None),
            P(),
            P("gx", "gy", None, None, None),
            P("gx", "gy", None),
            P("gx", "gy", None, None),
            P("gx", "gy", None),
            P("gx", "gy", None, None, None),
            P("gx", "gy", None, None),
        ),
        out_specs=(P("gx", "gy", None, None, None), P("gx", "gy", None, None, None), P("gx", None)),
        check_vma=False,
    )
```

profile of v0, /device:TPU:97, one launch (start us, length us, event | category | flops | bytes accessed | tf_op | source)
XLA Modules:
  0.0 1029.5 jit_solution(4450963363016071230)
XLA Ops:
  20.2 23.2 %slice.156 = bf16[3,5,5,5,192]{4,3,2,1,0:T(8,128)(2,1)} slice(bf16[3,11,11,11,192]{4,3,2,1,0:T(8,128)(2,1)S(1)} %pad.18), slice={[0:3:1], [0:9:2], [0:9:2], [0:9:2], [0:192:1]} | slice | bytes 288000 | tf_op jit(solution)/shard_map/vmap()/slice | solution.py:63
  43.4 23.0 %slice.157 = bf16[3,5,5,5,192]{4,3,2,1,0:T(8,128)(2,1)} slice(bf16[3,11,11,11,192]{4,3,2,1,0:T(8,128)(2,1)S(1)} %pad.18), slice={[0:3:1], [0:9:2], [0:9:2], [1:10:2], [0:192:1]} | slice | bytes 288000 | tf_op jit(solution)/shard_map/vmap()/slice | solution.py:63
  66.4 23.1 %slice.158 = bf16[3,5,5,5,192]{4,3,2,1,0:T(8,128)(2,1)} slice(bf16[3,11,11,11,192]{4,3,2,1,0:T(8,128)(2,1)S(1)} %pad.18), slice={[0:3:1], [0:9:2], [0:9:2], [2:11:2], [0:192:1]} | slice | bytes 288000 | tf_op jit(solution)/shard_map/vmap()/slice | solution.py:63
  89.5 23.0 %slice.159 = bf16[3,5,5,5,192]{4,3,2,1,0:T(8,128)(2,1)} slice(bf16[3,11,11,11,192]{4,3,2,1,0:T(8,128)(2,1)S(1)} %pad.18), slice={[0:3:1], [0:9:2], [1:10:2], [0:9:2], [0:192:1]} | slice | bytes 288000 | tf_op jit(solution)/shard_map/vmap()/slice | solution.py:63
  112.5 23.0 %slice.160 = bf16[3,5,5,5,192]{4,3,2,1,0:T(8,128)(2,1)} slice(bf16[3,11,11,11,192]{4,3,2,1,0:T(8,128)(2,1)S(1)} %pad.18), slice={[0:3:1], [0:9:2], [1:10:2], [1:10:2], [0:192:1]} | slice | bytes 288000 | tf_op jit(solution)/shard_map/vmap()/slice | solution.py:63
  135.5 23.0 %slice.161 = bf16[3,5,5,5,192]{4,3,2,1,0:T(8,128)(2,1)} slice(bf16[3,11,11,11,192]{4,3,2,1,0:T(8,128)(2,1)S(1)} %pad.18), slice={[0:3:1], [0:9:2], [1:10:2], [2:11:2], [0:192:1]} | slice | bytes 288000 | tf_op jit(solution)/shard_map/vmap()/slice | solution.py:63
  181.5 23.0 %slice.163 = bf16[3,5,5,5,192]{4,3,2,1,0:T(8,128)(2,1)} slice(bf16[3,11,11,11,192]{4,3,2,1,0:T(8,128)(2,1)S(1)} %pad.18), slice={[0:3:1], [0:9:2], [2:11:2], [1:10:2], [0:192:1]} | slice | bytes 288000 | tf_op jit(solution)/shard_map/vmap()/slice | solution.py:63
  227.5 23.0 %slice.165 = bf16[3,5,5,5,192]{4,3,2,1,0:T(8,128)(2,1)} slice(bf16[3,11,11,11,192]{4,3,2,1,0:T(8,128)(2,1)S(1)} %pad.18), slice={[0:3:1], [1:10:2], [0:9:2], [0:9:2], [0:192:1]} | slice | bytes 288000 | tf_op jit(solution)/shard_map/vmap()/slice | solution.py:63
  250.5 23.0 %slice.166 = bf16[3,5,5,5,192]{4,3,2,1,0:T(8,128)(2,1)} slice(bf16[3,11,11,11,192]{4,3,2,1,0:T(8,128)(2,1)S(1)} %pad.18), slice={[0:3:1], [1:10:2], [0:9:2], [1:10:2], [0:192:1]} | slice | bytes 288000 | tf_op jit(solution)/shard_map/vmap()/slice | solution.py:63
  273.5 23.0 %slice.167 = bf16[3,5,5,5,192]{4,3,2,1,0:T(8,128)(2,1)} slice(bf16[3,11,11,11,192]{4,3,2,1,0:T(8,128)(2,1)S(1)} %pad.18), slice={[0:3:1], [1:10:2], [0:9:2], [2:11:2], [0:192:1]} | slice | bytes 288000 | tf_op jit(solution)/shard_map/vmap()/slice | solution.py:63
  296.6 23.0 %slice.168 = bf16[3,5,5,5,192]{4,3,2,1,0:T(8,128)(2,1)} slice(bf16[3,11,11,11,192]{4,3,2,1,0:T(8,128)(2,1)S(1)} %pad.18), slice={[0:3:1], [1:10:2], [1:10:2], [0:9:2], [0:192:1]} | slice | bytes 288000 | tf_op jit(solution)/shard_map/vmap()/slice | solution.py:63
  319.6 23.0 %slice.169 = bf16[3,5,5,5,192]{4,3,2,1,0:T(8,128)(2,1)} slice(bf16[3,11,11,11,192]{4,3,2,1,0:T(8,128)(2,1)S(1)} %pad.18), slice={[0:3:1], [1:10:2], [1:10:2], [1:10:2], [0:192:1]} | slice | bytes 288000 | tf_op jit(solution)/shard_map/vmap()/slice | solution.py:63
  342.6 23.0 %slice.170 = bf16[3,5,5,5,192]{4,3,2,1,0:T(8,128)(2,1)} slice(bf16[3,11,11,11,192]{4,3,2,1,0:T(8,128)(2,1)S(1)} %pad.18), slice={[0:3:1], [1:10:2], [1:10:2], [2:11:2], [0:192:1]} | slice | bytes 288000 | tf_op jit(solution)/shard_map/vmap()/slice | solution.py:63
  365.6 23.0 %slice.171 = bf16[3,5,5,5,192]{4,3,2,1,0:T(8,128)(2,1)} slice(bf16[3,11,11,11,192]{4,3,2,1,0:T(8,128)(2,1)S(1)} %pad.18), slice={[0:3:1], [1:10:2], [2:11:2], [0:9:2], [0:192:1]} | slice | bytes 288000 | tf_op jit(solution)/shard_map/vmap()/slice | solution.py:63
  388.7 23.0 %slice.172 = bf16[3,5,5,5,192]{4,3,2,1,0:T(8,128)(2,1)} slice(bf16[3,11,11,11,192]{4,3,2,1,0:T(8,128)(2,1)S(1)} %pad.18), slice={[0:3:1], [1:10:2], [2:11:2], [1:10:2], [0:192:1]} | slice | bytes 288000 | tf_op jit(solution)/shard_map/vmap()/slice | solution.py:63
  411.7 23.0 %slice.173 = bf16[3,5,5,5,192]{4,3,2,1,0:T(8,128)(2,1)} slice(bf16[3,11,11,11,192]{4,3,2,1,0:T(8,128)(2,1)S(1)} %pad.18), slice={[0:3:1], [1:10:2], [2:11:2], [2:11:2], [0:192:1]} | slice | bytes 288000 | tf_op jit(solution)/shard_map/vmap()/slice | solution.py:63
  434.7 23.0 %slice.174 = bf16[3,5,5,5,192]{4,3,2,1,0:T(8,128)(2,1)} slice(bf16[3,11,11,11,192]{4,3,2,1,0:T(8,128)(2,1)S(1)} %pad.18), slice={[0:3:1], [2:11:2], [0:9:2], [0:9:2], [0:192:1]} | slice | bytes 288000 | tf_op jit(solution)/shard_map/vmap()/slice | solution.py:63
  457.7 23.0 %slice.175 = bf16[3,5,5,5,192]{4,3,2,1,0:T(8,128)(2,1)} slice(bf16[3,11,11,11,192]{4,3,2,1,0:T(8,128)(2,1)S(1)} %pad.18), slice={[0:3:1], [2:11:2], [0:9:2], [1:10:2], [0:192:1]} | slice | bytes 288000 | tf_op jit(solution)/shard_map/vmap()/slice | solution.py:63
  480.7 23.0 %slice.176 = bf16[3,5,5,5,192]{4,3,2,1,0:T(8,128)(2,1)} slice(bf16[3,11,11,11,192]{4,3,2,1,0:T(8,128)(2,1)S(1)} %pad.18), slice={[0:3:1], [2:11:2], [0:9:2], [2:11:2], [0:192:1]} | slice | bytes 288000 | tf_op jit(solution)/shard_map/vmap()/slice | solution.py:63
  503.7 23.0 %slice.177 = bf16[3,5,5,5,192]{4,3,2,1,0:T(8,128)(2,1)} slice(bf16[3,11,11,11,192]{4,3,2,1,0:T(8,128)(2,1)S(1)} %pad.18), slice={[0:3:1], [2:11:2], [1:10:2], [0:9:2], [0:192:1]} | slice | bytes 288000 | tf_op jit(solution)/shard_map/vmap()/slice | solution.py:63
  549.7 23.0 %slice.179 = bf16[3,5,5,5,192]{4,3,2,1,0:T(8,128)(2,1)} slice(bf16[3,11,11,11,192]{4,3,2,1,0:T(8,128)(2,1)S(1)} %pad.18), slice={[0:3:1], [2:11:2], [1:10:2], [2:11:2], [0:192:1]} | slice | bytes 288000 | tf_op jit(solution)/shard_map/vmap()/slice | solution.py:63
  572.7 23.0 %slice.180 = bf16[3,5,5,5,192]{4,3,2,1,0:T(8,128)(2,1)} slice(bf16[3,11,11,11,192]{4,3,2,1,0:T(8,128)(2,1)S(1)} %pad.18), slice={[0:3:1], [2:11:2], [2:11:2], [0:9:2], [0:192:1]} | slice | bytes 288000 | tf_op jit(solution)/shard_map/vmap()/slice | solution.py:63
  595.8 23.0 %slice.181 = bf16[3,5,5,5,192]{4,3,2,1,0:T(8,128)(2,1)} slice(bf16[3,11,11,11,192]{4,3,2,1,0:T(8,128)(2,1)S(1)} %pad.18), slice={[0:3:1], [2:11:2], [2:11:2], [1:10:2], [0:192:1]} | slice | bytes 288000 | tf_op jit(solution)/shard_map/vmap()/slice | solution.py:63
  776.3 244.7 %all-reduce.8.cloned.1.call-done = f32[5184,192]{1,0:T(8,128)} async-done(((f32[5184,192]{1,0:T(8,128)}), f32[5184,192]{1,0:T(8,128)}) %all-reduce.8.cloned.1.call-update) | async-done | bytes 3981328 | tf_op jit(solution)/shard_map/psum | solution.py:205
  (193 shorter events, 240.3 us)
Async XLA Ops:
  7.2 1013.9 %all-reduce.8.cloned.1.call-start = ((), (), s32[]{:S(2)}) async-start(), calls=%async_computation | async-start | bytes 10616832 | tf_op jit(solution)/shard_map/psum | solution.py:205
  8.6 691.1 %collective-permute-start = (s32[3]{0:T(128)}, s32[3]{0:T(128)}, u32[]{:S(2)}, u32[]{:S(2)}) collective-permute-start(s32[3]{0:T(128)} %get-tuple-element.12), channel_id=1, source_target_pairs={{0,8},{8,16},{16,24},{24,32},{32,40},{40,48},{48,56},{56,64},{64,7... | collective-permute-start | bytes 44 | tf_op jit(solution)/shard_map/ppermute | solution.py:12
  11.0 691.7 %collective-permute-start.2 = (s32[3]{0:T(128)}, s32[3]{0:T(128)}, u32[]{:S(2)}, u32[]{:S(2)}) collective-permute-start(s32[3]{0:T(128)} %get-tuple-element.14), channel_id=1, source_target_pairs={{0,1},{1,2},{2,3},{3,4},{4,5},{5,6},{6,7},{8,9},{9,10},{10,11},{11... | collective-permute-start | bytes 44 | tf_op jit(solution)/shard_map/ppermute | solution.py:12
  14.6 679.1 %collective-permute-start.4 = (s32[3]{0:T(128)}, s32[3]{0:T(128)}, u32[]{:S(2)}, u32[]{:S(2)}) collective-permute-start(s32[3]{0:T(128)} %get-tuple-element.17), channel_id=1, source_target_pairs={{0,8},{8,16},{16,24},{24,32},{32,40},{40,48},{48,56},{56,64},{64,7... | collective-permute-start | bytes 44 | tf_op jit(solution)/shard_map/ppermute | solution.py:12
  20.2 601.6 %copy-start.20 = (s32[1,1,3,3]{3,1,2,0:T(1,128)S(1)}, s32[1,1,3,3]{3,1,2,0:T(1,128)}, u32[]{:S(2)}) copy-start(s32[1,1,3,3]{3,1,2,0:T(1,128)} %param.19) | copy-start | bytes 112
  621.9 14.5 %copy-start.2 = (bf16[3,5,5,5,192]{4,3,2,1,0:T(8,128)(2,1)S(1)}, bf16[3,5,5,5,192]{4,3,2,1,0:T(8,128)(2,1)}, u32[]{:S(2)}) copy-start(bf16[3,5,5,5,192]{4,3,2,1,0:T(8,128)(2,1)} %slice.180) | copy-start | bytes 432004
  622.0 14.5 %copy-start.1 = (bf16[3,5,5,5,192]{4,3,2,1,0:T(8,128)(2,1)S(1)}, bf16[3,5,5,5,192]{4,3,2,1,0:T(8,128)(2,1)}, u32[]{:S(2)}) copy-start(bf16[3,5,5,5,192]{4,3,2,1,0:T(8,128)(2,1)} %slice.181) | copy-start | bytes 432004
  641.3 17.4 %copy-start.22 = (s32[1,1,12]{2,1,0:T(1,128)S(1)}, s32[1,1,12]{2,1,0:T(1,128)}, u32[]{:S(2)}) copy-start(s32[1,1,12]{2,1,0:T(1,128)} %param.17) | copy-start | bytes 148
  641.3 17.5 %copy-start.17 = (s32[8,16]{1,0:T(8,128)S(1)}, s32[8,16]{1,0:T(8,128)}, u32[]{:S(2)}) copy-start(s32[8,16]{1,0:T(8,128)} %constant.34.clone) | copy-start | bytes 1540
  641.3 24.5 %copy-start.15 = (bf16[1,1,3,64,192]{4,3,2,1,0:T(8,128)(2,1)S(1)}, bf16[1,1,3,64,192]{4,3,2,1,0:T(8,128)(2,1)}, u32[]{:S(2)}) copy-start(bf16[1,1,3,64,192]{4,3,2,1,0:T(8,128)(2,1)} %param.14) | copy-start | bytes 221188
  655.5 64.0 %collective-permute-start.3 = (bf16[3,16,192]{2,1,0:T(8,128)(2,1)S(1)}, bf16[3,16,192]{2,1,0:T(8,128)(2,1)}, u32[]{:S(2)}, u32[]{:S(2)}) collective-permute-start(bf16[3,16,192]{2,1,0:T(8,128)(2,1)S(1)} %convolution_convert_fusion.3), channel_id=1, source_target_pairs={{0,1},{1,2},{2,3},{3,4},{4,5},{5,6},{6,7},{8,9},{9,10},{10,11},{11... | collective-permute-start | bytes 55304 | tf_op jit(solution)/shard_map/ppermute | solution.py:12
  660.3 21.1 %copy-start.16 = (s32[8,4]{1,0:T(8,128)S(1)}, s32[8,4]{1,0:T(8,128)}, u32[]{:S(2)}) copy-start(s32[8,4]{1,0:T(8,128)} %constant.36.clone) | copy-start | bytes 388
  660.3 60.1 %collective-permute-start.1 = (bf16[3,16,192]{2,1,0:T(8,128)(2,1)}, bf16[3,16,192]{2,1,0:T(8,128)(2,1)}, u32[]{:S(2)}, u32[]{:S(2)}) collective-permute-start(bf16[3,16,192]{2,1,0:T(8,128)(2,1)} %convolution_convert_fusion.4), channel_id=1, source_target_pairs={{0,8},{8,16},{16,24},{24,32},{32,40},{40,48},{48,56},{56,64},{64,7... | collective-permute-start | bytes 55304 | tf_op jit(solution)/shard_map/ppermute | solution.py:12
  665.8 19.2 %copy-start.13 = (s32[8,64]{1,0:T(8,128)S(1)}, s32[8,64]{1,0:T(8,128)}, u32[]{:S(2)}) copy-start(s32[8,64]{1,0:T(8,128)} %constant.37.clone) | copy-start | bytes 6148
  666.7 19.0 %slice-start = ((bf16[4,4,4,4,192]{4,3,2,1,0:T(4,128)(2,1)}), bf16[4,1,4,4,192]{4,3,2,1,0:T(4,128)(2,1)S(1)}, s32[]{:S(2)}) async-start(bf16[4,4,4,4,192]{4,3,2,1,0:T(4,128)(2,1)} %copy-done.14), calls=%async_computation.1 | async-start | bytes 65536 | tf_op jit(solution)/shard_map/slice | solution.py:170
  666.8 19.7 %slice-start.1 = ((bf16[4,4,4,4,192]{4,3,2,1,0:T(4,128)(2,1)}), bf16[4,4,1,4,192]{4,3,2,1,0:T(4,128)(2,1)S(1)}, s32[]{:S(2)}) async-start(bf16[4,4,4,4,192]{4,3,2,1,0:T(4,128)(2,1)} %copy-done.14), calls=%async_computation.2 | async-start | bytes 65536 | tf_op jit(solution)/shard_map/slice | solution.py:171
  693.7 3.1 collective-permute-start.5
  696.8 23.5 %copy-start.21 = (s32[3]{0:T(128)}, s32[3]{0:T(128)S(1)}, u32[]{:S(2)}) copy-start(s32[3]{0:T(128)S(1)} %collective-permute-done.5) | copy-start | bytes 40
  696.8 14.4 %collective-permute-start.6 = (f32[3,4,192]{2,1,0:T(4,128)}, f32[3,4,192]{2,1,0:T(4,128)}, u32[]{:S(2)}, u32[]{:S(2)}) collective-permute-start(f32[3,4,192]{2,1,0:T(4,128)} %fusion.28), channel_id=1, source_target_pairs={{0,8},{8,16},{16,24},{24,32},{32,40},{40,48},{48,56},{56,64},{64,7... | collective-permute-start | bytes 27656 | tf_op jit(solution)/shard_map/ppermute | solution.py:12
  699.7 9.1 collective-permute-start.10
  702.7 24.2 %collective-permute-start.8 = (bf16[3,16,192]{2,1,0:T(8,128)(2,1)}, bf16[3,16,192]{2,1,0:T(8,128)(2,1)}, u32[]{:S(2)}, u32[]{:S(2)}) collective-permute-start(bf16[3,16,192]{2,1,0:T(8,128)(2,1)} %reshape.429), channel_id=1, source_target_pairs={{8,0},{16,8},{24,16},{32,24},{40,32},{48,40},{56,48},{64,56},{72,6... | collective-permute-start | bytes 55304 | tf_op jit(solution)/shard_map/ppermute | solution.py:12
  708.9 9.3 collective-permute-start.11
  711.2 10.2 collective-permute-start.7
  718.2 8.6 collective-permute-start.9
  (14 other events, 168.5 us)
Sparse Core Ops, SparseCore 0:
  735.2 285.8 all-reduce.7
where the time goes:
time: 1030 us
  local copies, waits for them, and re-layouts  683 us (66%)
  waiting for transfers between devices  250 us (24%)
  starting transfers between devices  32.8 us (3%)
  matrix products  27.9 us (3%)
  other arithmetic  20.6 us (2%)
  between operations  14.9 us (1%)
    slice x27, local copies, waits for them, and re-layouts, brick_patches(): padded[along_x:along_x + 9:2, along_y:along_y + 9:2, along_z:along_z + 9:...  602 us
    psum x1, waiting for transfers between devices, shards(): summed = lax.psum(weight_local, ('gx', 'gy'))  245 us
    ppermute x12, starting transfers between devices, shifted(): return lax.ppermute(block, axis, route)  32.8 us
    unnamed x76, local copies, waits for them, and re-layouts  21.5 us
  transfers between devices with their start and end apart: 13, of which 3 were waited for; matrix products, arithmetic and copies ran while one was open for 70% of the time, Pallas kernels for 0%

commit v1 on v0

--- a/solution.py
+++ b/solution.py
@@ -202,7 +202,9 @@
         patch_grads.reshape(bricks, 125, 27 * channels)
     )
     features_grad = (folded * live_float).astype(jnp.bfloat16)
-    summed = lax.psum(weight_local, ("gx", "gy"))
+    summed = weight_local
+    for mesh_axis in ("gx", "gy"):
+        summed = lax.psum(summed, mesh_axis)
     share_rows = summed.shape[0] // lax.axis_size("gx")
     weight_share = lax.dynamic_slice_in_dim(
         summed, lax.axis_index("gx") * share_rows, share_rows, 0

time: 1030 us -> 1260 us (1.22); the launches traced: 1030 us -> 1250 us
  waiting for transfers between devices: 250 us -> 446 us
  local copies, waits for them, and re-layouts: 683 us -> 701 us
    psum x1 -> x2, waiting for transfers between devices: 245 us -> 443 us  [shards(): summed = lax.psum(summed, mesh_axis)]
    unnamed x76 -> x84, local copies, waits for them, and re-layouts: 21.5 us -> 39.2 us
  transfers between devices with their start and end apart: 13 -> 14, of which waited for: 3 -> 4; matrix products, arithmetic and copies ran while one was open for 70% -> 59% of each run, Pallas kernels for 0% -> 0%
where the time goes in v1:
time: 1260 us; the launch traced here: 1250 us
  local copies, waits for them, and re-layouts  701 us (56%)
  waiting for transfers between devices  446 us (35%)
  starting transfers between devices  40.4 us (3%)
  matrix products  24.2 us (2%)
  other arithmetic  18.7 us (1%)
  between operations  14.8 us (1%)
    slice x27, local copies, waits for them, and re-layouts, brick_patches(): padded[along_x:along_x + 9:2, along_y:along_y + 9:2, along_z:along_z + 9:...  602 us
    psum x2, waiting for transfers between devices, shards(): summed = lax.psum(summed, mesh_axis)  443 us
    ppermute x12, starting transfers between devices, shifted(): return lax.ppermute(block, axis, route)  40.2 us
    unnamed x84, local copies, waits for them, and re-layouts  39.2 us
  transfers between devices with their start and end apart: 14, of which 4 were waited for; matrix products, arithmetic and copies ran while one was open for 59% of the time, Pallas kernels for 0%

profile of v1, /device:TPU:97, one launch (start us, length us, event | category | flops | bytes accessed | tf_op | source)
XLA Modules:
  0.0 1245.2 jit_solution(2619998340919093440)
XLA Ops:
  20.4 23.2 %slice.156 = bf16[3,5,5,5,192]{4,3,2,1,0:T(8,128)(2,1)} slice(bf16[3,11,11,11,192]{4,3,2,1,0:T(8,128)(2,1)S(1)} %pad.18), slice={[0:3:1], [0:9:2], [0:9:2], [0:9:2], [0:192:1]} | slice | bytes 288000 | tf_op jit(solution)/shard_map/vmap()/slice | solution.py:63
  43.6 23.0 %slice.157 = bf16[3,5,5,5,192]{4,3,2,1,0:T(8,128)(2,1)} slice(bf16[3,11,11,11,192]{4,3,2,1,0:T(8,128)(2,1)S(1)} %pad.18), slice={[0:3:1], [0:9:2], [0:9:2], [1:10:2], [0:192:1]} | slice | bytes 288000 | tf_op jit(solution)/shard_map/vmap()/slice | solution.py:63
  66.6 23.0 %slice.158 = bf16[3,5,5,5,192]{4,3,2,1,0:T(8,128)(2,1)} slice(bf16[3,11,11,11,192]{4,3,2,1,0:T(8,128)(2,1)S(1)} %pad.18), slice={[0:3:1], [0:9:2], [0:9:2], [2:11:2], [0:192:1]} | slice | bytes 288000 | tf_op jit(solution)/shard_map/vmap()/slice | solution.py:63
  89.6 23.0 %slice.159 = bf16[3,5,5,5,192]{4,3,2,1,0:T(8,128)(2,1)} slice(bf16[3,11,11,11,192]{4,3,2,1,0:T(8,128)(2,1)S(1)} %pad.18), slice={[0:3:1], [0:9:2], [1:10:2], [0:9:2], [0:192:1]} | slice | bytes 288000 | tf_op jit(solution)/shard_map/vmap()/slice | solution.py:63
  112.7 23.0 %slice.160 = bf16[3,5,5,5,192]{4,3,2,1,0:T(8,128)(2,1)} slice(bf16[3,11,11,11,192]{4,3,2,1,0:T(8,128)(2,1)S(1)} %pad.18), slice={[0:3:1], [0:9:2], [1:10:2], [1:10:2], [0:192:1]} | slice | bytes 288000 | tf_op jit(solution)/shard_map/vmap()/slice | solution.py:63
  135.7 23.0 %slice.161 = bf16[3,5,5,5,192]{4,3,2,1,0:T(8,128)(2,1)} slice(bf16[3,11,11,11,192]{4,3,2,1,0:T(8,128)(2,1)S(1)} %pad.18), slice={[0:3:1], [0:9:2], [1:10:2], [2:11:2], [0:192:1]} | slice | bytes 288000 | tf_op jit(solution)/shard_map/vmap()/slice | solution.py:63
  158.7 23.0 %slice.162 = bf16[3,5,5,5,192]{4,3,2,1,0:T(8,128)(2,1)} slice(bf16[3,11,11,11,192]{4,3,2,1,0:T(8,128)(2,1)S(1)} %pad.18), slice={[0:3:1], [0:9:2], [2:11:2], [0:9:2], [0:192:1]} | slice | bytes 288000 | tf_op jit(solution)/shard_map/vmap()/slice | solution.py:63
  181.7 23.0 %slice.163 = bf16[3,5,5,5,192]{4,3,2,1,0:T(8,128)(2,1)} slice(bf16[3,11,11,11,192]{4,3,2,1,0:T(8,128)(2,1)S(1)} %pad.18), slice={[0:3:1], [0:9:2], [2:11:2], [1:10:2], [0:192:1]} | slice | bytes 288000 | tf_op jit(solution)/shard_map/vmap()/slice | solution.py:63
  227.8 23.0 %slice.165 = bf16[3,5,5,5,192]{4,3,2,1,0:T(8,128)(2,1)} slice(bf16[3,11,11,11,192]{4,3,2,1,0:T(8,128)(2,1)S(1)} %pad.18), slice={[0:3:1], [1:10:2], [0:9:2], [0:9:2], [0:192:1]} | slice | bytes 288000 | tf_op jit(solution)/shard_map/vmap()/slice | solution.py:63
  250.8 23.1 %slice.166 = bf16[3,5,5,5,192]{4,3,2,1,0:T(8,128)(2,1)} slice(bf16[3,11,11,11,192]{4,3,2,1,0:T(8,128)(2,1)S(1)} %pad.18), slice={[0:3:1], [1:10:2], [0:9:2], [1:10:2], [0:192:1]} | slice | bytes 288000 | tf_op jit(solution)/shard_map/vmap()/slice | solution.py:63
  273.8 23.1 %slice.167 = bf16[3,5,5,5,192]{4,3,2,1,0:T(8,128)(2,1)} slice(bf16[3,11,11,11,192]{4,3,2,1,0:T(8,128)(2,1)S(1)} %pad.18), slice={[0:3:1], [1:10:2], [0:9:2], [2:11:2], [0:192:1]} | slice | bytes 288000 | tf_op jit(solution)/shard_map/vmap()/slice | solution.py:63
  296.9 23.0 %slice.168 = bf16[3,5,5,5,192]{4,3,2,1,0:T(8,128)(2,1)} slice(bf16[3,11,11,11,192]{4,3,2,1,0:T(8,128)(2,1)S(1)} %pad.18), slice={[0:3:1], [1:10:2], [1:10:2], [0:9:2], [0:192:1]} | slice | bytes 288000 | tf_op jit(solution)/shard_map/vmap()/slice | solution.py:63
  319.9 23.0 %slice.169 = bf16[3,5,5,5,192]{4,3,2,1,0:T(8,128)(2,1)} slice(bf16[3,11,11,11,192]{4,3,2,1,0:T(8,128)(2,1)S(1)} %pad.18), slice={[0:3:1], [1:10:2], [1:10:2], [1:10:2], [0:192:1]} | slice | bytes 288000 | tf_op jit(solution)/shard_map/vmap()/slice | solution.py:63
  342.9 23.0 %slice.170 = bf16[3,5,5,5,192]{4,3,2,1,0:T(8,128)(2,1)} slice(bf16[3,11,11,11,192]{4,3,2,1,0:T(8,128)(2,1)S(1)} %pad.18), slice={[0:3:1], [1:10:2], [1:10:2], [2:11:2], [0:192:1]} | slice | bytes 288000 | tf_op jit(solution)/shard_map/vmap()/slice | solution.py:63
  366.0 23.0 %slice.171 = bf16[3,5,5,5,192]{4,3,2,1,0:T(8,128)(2,1)} slice(bf16[3,11,11,11,192]{4,3,2,1,0:T(8,128)(2,1)S(1)} %pad.18), slice={[0:3:1], [1:10:2], [2:11:2], [0:9:2], [0:192:1]} | slice | bytes 288000 | tf_op jit(solution)/shard_map/vmap()/slice | solution.py:63
  389.0 23.1 %slice.172 = bf16[3,5,5,5,192]{4,3,2,1,0:T(8,128)(2,1)} slice(bf16[3,11,11,11,192]{4,3,2,1,0:T(8,128)(2,1)S(1)} %pad.18), slice={[0:3:1], [1:10:2], [2:11:2], [1:10:2], [0:192:1]} | slice | bytes 288000 | tf_op jit(solution)/shard_map/vmap()/slice | solution.py:63
  412.1 23.0 %slice.173 = bf16[3,5,5,5,192]{4,3,2,1,0:T(8,128)(2,1)} slice(bf16[3,11,11,11,192]{4,3,2,1,0:T(8,128)(2,1)S(1)} %pad.18), slice={[0:3:1], [1:10:2], [2:11:2], [2:11:2], [0:192:1]} | slice | bytes 288000 | tf_op jit(solution)/shard_map/vmap()/slice | solution.py:63
  435.1 23.0 %slice.174 = bf16[3,5,5,5,192]{4,3,2,1,0:T(8,128)(2,1)} slice(bf16[3,11,11,11,192]{4,3,2,1,0:T(8,128)(2,1)S(1)} %pad.18), slice={[0:3:1], [2:11:2], [0:9:2], [0:9:2], [0:192:1]} | slice | bytes 288000 | tf_op jit(solution)/shard_map/vmap()/slice | solution.py:63
  504.1 23.0 %slice.177 = bf16[3,5,5,5,192]{4,3,2,1,0:T(8,128)(2,1)} slice(bf16[3,11,11,11,192]{4,3,2,1,0:T(8,128)(2,1)S(1)} %pad.18), slice={[0:3:1], [2:11:2], [1:10:2], [0:9:2], [0:192:1]} | slice | bytes 288000 | tf_op jit(solution)/shard_map/vmap()/slice | solution.py:63
  527.1 23.0 %slice.178 = bf16[3,5,5,5,192]{4,3,2,1,0:T(8,128)(2,1)} slice(bf16[3,11,11,11,192]{4,3,2,1,0:T(8,128)(2,1)S(1)} %pad.18), slice={[0:3:1], [2:11:2], [1:10:2], [1:10:2], [0:192:1]} | slice | bytes 288000 | tf_op jit(solution)/shard_map/vmap()/slice | solution.py:63
  550.1 23.0 %slice.179 = bf16[3,5,5,5,192]{4,3,2,1,0:T(8,128)(2,1)} slice(bf16[3,11,11,11,192]{4,3,2,1,0:T(8,128)(2,1)S(1)} %pad.18), slice={[0:3:1], [2:11:2], [1:10:2], [2:11:2], [0:192:1]} | slice | bytes 288000 | tf_op jit(solution)/shard_map/vmap()/slice | solution.py:63
  573.2 23.0 %slice.180 = bf16[3,5,5,5,192]{4,3,2,1,0:T(8,128)(2,1)} slice(bf16[3,11,11,11,192]{4,3,2,1,0:T(8,128)(2,1)S(1)} %pad.18), slice={[0:3:1], [2:11:2], [2:11:2], [0:9:2], [0:192:1]} | slice | bytes 288000 | tf_op jit(solution)/shard_map/vmap()/slice | solution.py:63
  746.6 247.8 %all-reduce.9.cloned.1.call-done = f32[5184,192]{1,0:T(8,128)} async-done(((f32[5184,192]{1,0:T(8,128)}), f32[5184,192]{1,0:T(8,128)}) %all-reduce.9.cloned.1.call-update) | async-done | bytes 3981328 | tf_op jit(solution)/shard_map/psum | solution.py:207
  1041.4 195.4 %all-reduce.11.cloned.1.call-done = f32[5184,192]{1,0:T(8,128)} async-done(((f32[5184,192]{1,0:T(8,128)}), f32[5184,192]{1,0:T(8,128)}) %all-reduce.11.cloned.1.call-update) | async-done | bytes 3981328 | tf_op jit(solution)/shard_map/psum | solution.py:207
  (202 shorter events, 280.5 us)
Async XLA Ops:
  7.2 987.2 %all-reduce.9.cloned.1.call-start = ((), (), s32[]{:S(2)}) async-start(), calls=%async_computation | async-start | bytes 10616832 | tf_op jit(solution)/shard_map/psum | solution.py:207
  8.0 650.9 %collective-permute-start = (s32[3]{0:T(128)S(1)}, s32[3]{0:T(128)S(1)}, u32[]{:S(2)}, u32[]{:S(2)}) collective-permute-start(s32[3]{0:T(128)S(1)} %get-tuple-element.12), channel_id=1, source_target_pairs={{0,8},{8,16},{16,24},{24,32},{32,40},{40,48},{48,56},{56,64},{64,7... | collective-permute-start | bytes 44 | tf_op jit(solution)/shard_map/ppermute | solution.py:12
  10.4 656.3 %collective-permute-start.2 = (s32[3]{0:T(128)S(1)}, s32[3]{0:T(128)S(1)}, u32[]{:S(2)}, u32[]{:S(2)}) collective-permute-start(s32[3]{0:T(128)S(1)} %get-tuple-element.14), channel_id=1, source_target_pairs={{0,1},{1,2},{2,3},{3,4},{4,5},{5,6},{6,7},{8,9},{9,10},{10,11},{11... | collective-permute-start | bytes 44 | tf_op jit(solution)/shard_map/ppermute | solution.py:12
  13.5 647.8 %collective-permute-start.4 = (s32[3]{0:T(128)S(1)}, s32[3]{0:T(128)S(1)}, u32[]{:S(2)}, u32[]{:S(2)}) collective-permute-start(s32[3]{0:T(128)S(1)} %get-tuple-element.17), channel_id=1, source_target_pairs={{0,8},{8,16},{16,24},{24,32},{32,40},{40,48},{48,56},{56,64},{64,7... | collective-permute-start | bytes 44 | tf_op jit(solution)/shard_map/ppermute | solution.py:12
  20.4 601.9 %copy-start.21 = (s32[1,1,3,3]{3,1,2,0:T(1,128)S(1)}, s32[1,1,3,3]{3,1,2,0:T(1,128)}, u32[]{:S(2)}) copy-start(s32[1,1,3,3]{3,1,2,0:T(1,128)} %param.19) | copy-start | bytes 112
  20.4 602.0 %copy-start.18 = (s32[8,16]{1,0:T(8,128)S(1)}, s32[8,16]{1,0:T(8,128)}, u32[]{:S(2)}) copy-start(s32[8,16]{1,0:T(8,128)} %constant.35.clone) | copy-start | bytes 1540
  20.4 602.7 %copy-start.17 = (s32[8,4]{1,0:T(8,128)S(1)}, s32[8,4]{1,0:T(8,128)}, u32[]{:S(2)}) copy-start(s32[8,4]{1,0:T(8,128)} %constant.36.clone) | copy-start | bytes 388
  20.4 603.4 %copy-start.26 = (s32[1,1,12]{2,1,0:T(1,128)S(1)}, s32[1,1,12]{2,1,0:T(1,128)}, u32[]{:S(2)}) copy-start(s32[1,1,12]{2,1,0:T(1,128)} %param.17) | copy-start | bytes 148
  20.4 603.4 %copy-start.16 = (s32[8,16]{1,0:T(8,128)S(1)}, s32[8,16]{1,0:T(8,128)}, u32[]{:S(2)}) copy-start(s32[8,16]{1,0:T(8,128)} %constant.34.clone) | copy-start | bytes 1540
  20.4 604.2 %copy-start.22 = (s32[1,1,2,12]{3,2,1,0:T(2,128)S(1)}, s32[1,1,2,12]{3,2,1,0:T(2,128)}, u32[]{:S(2)}) copy-start(s32[1,1,2,12]{3,2,1,0:T(2,128)} %param.16) | copy-start | bytes 292
  20.4 604.2 %copy-start.15 = (s32[8,64]{1,0:T(8,128)S(1)}, s32[8,64]{1,0:T(8,128)}, u32[]{:S(2)}) copy-start(s32[8,64]{1,0:T(8,128)} %constant.37.clone) | copy-start | bytes 6148
  622.3 34.2 %copy-start.3 = (bf16[3,5,5,5,192]{4,3,2,1,0:T(8,128)(2,1)S(1)}, bf16[3,5,5,5,192]{4,3,2,1,0:T(8,128)(2,1)}, u32[]{:S(2)}) copy-start(bf16[3,5,5,5,192]{4,3,2,1,0:T(8,128)(2,1)} %slice.180) | copy-start | bytes 432004
  622.3 35.0 %copy-start.2 = (bf16[3,5,5,5,192]{4,3,2,1,0:T(8,128)(2,1)S(1)}, bf16[3,5,5,5,192]{4,3,2,1,0:T(8,128)(2,1)}, u32[]{:S(2)}) copy-start(bf16[3,5,5,5,192]{4,3,2,1,0:T(8,128)(2,1)} %slice.181) | copy-start | bytes 432004
  658.8 35.4 %copy-start.23 = (s32[3]{0:T(128)}, s32[3]{0:T(128)S(1)}, u32[]{:S(2)}) copy-start(s32[3]{0:T(128)S(1)} %collective-permute-done) | copy-start | bytes 40
  659.1 35.1 %collective-permute-start.8 = (bf16[3,16,192]{2,1,0:T(8,128)(2,1)S(1)}, bf16[3,16,192]{2,1,0:T(8,128)(2,1)S(1)}, u32[]{:S(2)}, u32[]{:S(2)}) collective-permute-start(bf16[3,16,192]{2,1,0:T(8,128)(2,1)S(1)} %reshape.429), channel_id=1, source_target_pairs={{8,0},{16,8},{24,16},{32,24},{40,32},{48,40},{56,48},{64,56},{72,6... | collective-permute-start | bytes 55304 | tf_op jit(solution)/shard_map/ppermute | solution.py:12
  661.3 3.8 collective-permute-start.5
  665.4 4.6 collective-permute-start.10
  667.0 27.3 %collective-permute-start.9 = (bf16[3,16,192]{2,1,0:T(8,128)(2,1)S(1)}, bf16[3,16,192]{2,1,0:T(8,128)(2,1)S(1)}, u32[]{:S(2)}, u32[]{:S(2)}) collective-permute-start(bf16[3,16,192]{2,1,0:T(8,128)(2,1)S(1)} %reshape.431), channel_id=1, source_target_pairs={{1,0},{2,1},{3,2},{4,3},{5,4},{6,5},{7,6},{9,8},{10,9},{11,10},{12... | collective-permute-start | bytes 55304 | tf_op jit(solution)/shard_map/ppermute | solution.py:12
  670.0 24.2 %collective-permute-start.11 = (bf16[3,4,192]{2,1,0:T(4,128)(2,1)S(1)}, bf16[3,4,192]{2,1,0:T(4,128)(2,1)S(1)}, u32[]{:S(2)}, u32[]{:S(2)}) collective-permute-start(bf16[3,4,192]{2,1,0:T(4,128)(2,1)S(1)} %collective-permute-done.10), channel_id=1, source_target_pairs={{8,0},{16,8},{24,16},{32,24},{40,32},{48,40},{56,48},{64,56},{72,6... | collective-permute-start | bytes 13832 | tf_op jit(solution)/shard_map/ppermute | solution.py:12
  701.8 535.0 %all-reduce.11.cloned.1.call-start = ((), (), s32[]{:S(2)}) async-start(), calls=%async_computation.1 | async-start | bytes 10616832 | tf_op jit(solution)/shard_map/psum | solution.py:207
  715.6 27.6 %collective-permute-start.3 = (bf16[3,16,192]{2,1,0:T(8,128)(2,1)S(1)}, bf16[3,16,192]{2,1,0:T(8,128)(2,1)S(1)}, u32[]{:S(2)}, u32[]{:S(2)}) collective-permute-start(bf16[3,16,192]{2,1,0:T(8,128)(2,1)S(1)} %convolution_convert_fusion.3), channel_id=1, source_target_pairs={{0,1},{1,2},{2,3},{3,4},{4,5},{5,6},{6,7},{8,9},{9,10},{10,11},{11... | collective-permute-start | bytes 55304 | tf_op jit(solution)/shard_map/ppermute | solution.py:12
  721.8 9.1 collective-permute-start.6
  728.6 14.8 %collective-permute-start.1 = (bf16[3,16,192]{2,1,0:T(8,128)(2,1)S(1)}, bf16[3,16,192]{2,1,0:T(8,128)(2,1)}, u32[]{:S(2)}, u32[]{:S(2)}) collective-permute-start(bf16[3,16,192]{2,1,0:T(8,128)(2,1)S(1)} %convolution_convert_fusion.4), channel_id=1, source_target_pairs={{0,8},{8,16},{16,24},{24,32},{32,40},{40,48},{48,56},{56,64},{64,7... | collective-permute-start | bytes 55304 | tf_op jit(solution)/shard_map/ppermute | solution.py:12
  730.9 13.4 %collective-permute-start.7 = (f32[3,4,192]{2,1,0:T(4,128)}, f32[3,4,192]{2,1,0:T(4,128)}, u32[]{:S(2)}, u32[]{:S(2)}) collective-permute-start(f32[3,4,192]{2,1,0:T(4,128)} %collective-permute-done.6), channel_id=1, source_target_pairs={{0,1},{1,2},{2,3},{3,4},{4,5},{5,6},{6,7},{8,9},{9,10},{10,11},{11... | collective-permute-start | bytes 27656 | tf_op jit(solution)/shard_map/ppermute | solution.py:12
  (17 other events, 387.5 us)
Sparse Core Ops, SparseCore 0:
  701.9 292.4 all-reduce.8
  997.1 239.6 all-reduce.10
